TPU v7x, 32 devices: a whole 2x2x4 slice. The times are simulated.
32 devices in a mesh: dp: 4 (over x, core), expert: 8 (over z, y).
Axes of the slice: x: 2, y: 2, z: 4, core: 2. Of those that a mesh axis runs over, the one named last changes fastest.
Arguments:
- grad_partials: bfloat16 [4, 7168, 8192], P('dp', None, 'expert'), may hold values from -6 to 6
- master_weights: float32 [7168, 8192], P('dp', 'expert'), may hold values from -0.3125 to 0.3125
- first_moment: float32 [7168, 8192], P('dp', 'expert'), may hold values from -2 to 2
- second_moment: float32 [7168, 8192], P('dp', 'expert'), may hold values from 0.02 to 0.5
- resident_weights: bfloat16 [7168, 16384], P('dp', 'expert'), may hold values from -0.6 to 0.6
- token_tiles: bfloat16 [8192, 7168], P('expert', 'dp'), may hold values from -6 to 6
- owner_expert: int32 [8], replicated, may hold values from 0 to 3, as said below
- live_rows: int32 [8], P('expert'), may hold values from 256 to 1024, as said below
Outputs:
- updated_master: float32 [7168, 8192], P('dp', 'expert')
- projected: bfloat16 [8192, 2048], P('expert', 'dp')
Inputs may be any that keep to these rules, and one draw needn't show every extreme that they name: `owner_expert`: each owner hosts one of the 4 experts; every expert is hosted by at least one owner, some by several. The first live_rows[o] of owner o's rows are live; some owner has all 1024 rows live.
All inputs are finite; a program needn't handle non-finite values.
Results may differ from a plain program's by a relative error of at most 0.035.
Values may be sent and summed in bfloat16 or wider, within the bound.
No kernel may reach another device: no remote copies, remote signals or barrier semaphores. Data moves between devices by JAX's collectives and lax.ppermute only.
A program may use at most 192 MiB of HBM per device.

v0:
```python
import jax
import jax.numpy as jnp
from jax import lax
from jax.sharding import PartitionSpec as P

EXPERTS = 4
QB = 128
beta_first = 0.9
beta_second = 0.95
learn_rate = 0.02
decay_rate = 0.1
adam_epsilon = 1e-08
scale_epsilon = 1e-06
quant_range = 448.0
grid_step = 8.0
bias_first = 1.0 - 0.9**20
bias_second = 1.0 - 0.95**20


def adamw(gradient, master_weights, first_moment, second_moment):
    moment_one = beta_first * first_moment + (1.0 - beta_first) * gradient
    moment_two = beta_second * second_moment + (1.0 - beta_second) * gradient * gradient
    update = moment_one / bias_first / (jnp.sqrt(moment_two / bias_second) + adam_epsilon)
    return master_weights - learn_rate * (update + decay_rate * master_weights)


def block_product(stacked, weight):
    depth_blocks = stacked.shape[0]
    width_total = weight.shape[1]
    blocks = weight.reshape(depth_blocks, QB, width_total // QB, QB)
    largest = jnp.max(jnp.abs(blocks), axis=(1, 3))
    scales = (largest + scale_epsilon) / quant_range
    ratio = blocks / scales[:, None, :, None]
    level = grid_step * jnp.floor(ratio / grid_step + 0.5)
    quantized = level.astype(jnp.bfloat16).reshape(depth_blocks, QB, width_total)
    col_scales = jnp.repeat(scales, QB, axis=1)

    def step_block(running, inputs):
        tile_part, weight_part, scale_part = inputs
        product = jnp.dot(tile_part, weight_part, preferred_element_type=jnp.float32)
        return (running + product * scale_part[None, :], None)

    initial = jnp.zeros((stacked.shape[1], width_total), jnp.float32)
    result, unused = lax.scan(step_block, initial, (stacked, quantized, col_scales))
    return result


def body(
    grad_partials,
    master_weights,
    first_moment,
    second_moment,
    resident_weights,
    token_tiles,
    owner_expert,
    live_rows,
):
    gradient = lax.psum_scatter(
        grad_partials[0].astype(jnp.float32).astype(jnp.bfloat16),
        "dp",
        scatter_dimension=0,
        tiled=True,
    ).astype(jnp.float32)
    updated_master = adamw(gradient, master_weights, first_moment, second_moment)
    delta = (updated_master - master_weights).astype(jnp.bfloat16)
    group_size = lax.axis_size("expert") // EXPERTS
    own_index = lax.axis_index("expert")
    own_expert = owner_expert[own_index]
    rows_local = token_tiles.shape[0]
    depth_blocks = token_tiles.shape[1] // QB
    stacked = token_tiles.reshape(rows_local, depth_blocks, QB).transpose(1, 0, 2)
    part_cols = delta.shape[1]
    gathered = lax.all_gather(delta[None], "expert", axis=0, tiled=True)
    own_pieces = lax.dynamic_slice_in_dim(gathered, own_expert * group_size, group_size, 0)
    change = own_pieces.transpose(1, 0, 2).reshape(own_pieces.shape[1], group_size * part_cols)
    weight = resident_weights.astype(jnp.float32) + change.astype(jnp.float32)
    partial_out = block_product(stacked, weight)
    summed = lax.psum_scatter(
        partial_out.astype(jnp.bfloat16), "dp", scatter_dimension=1, tiled=True
    ).astype(jnp.float32)
    row_index = lax.broadcasted_iota(jnp.int32, summed.shape, 0)
    projected = jnp.where(row_index < live_rows[0], summed, jnp.float32(0.0)).astype(jnp.bfloat16)
    return (updated_master, projected)


def solution(mesh):
    placed = (
        P("dp", None, "expert"),
        P("dp", "expert"),
        P("dp", "expert"),
        P("dp", "expert"),
        P("dp", "expert"),
        P("expert", "dp"),
        P(),
        P("expert"),
    )
    return jax.shard_map(
        body,
        mesh=mesh,
        in_specs=placed,
        out_specs=(P("dp", "expert"), P("expert", "dp")),
        check_vma=False,
    )
```

profile of v0, /device:TPU:0, one launch (start us, length us, event | category | flops | bytes accessed | tf_op | source)
XLA Modules:
  0.0 945.2 jit_solution(4258799347159159431)
XLA Ops:
  8.0 119.3 %reduce-scatter.3.cloned.1.call-done = bf16[1792,1024]{1,0:T(8,128)(2,1)} async-done(((bf16[7168,1024]{1,0:T(8,128)(2,1)}), bf16[1792,1024]{1,0:T(8,128)(2,1)}) %reduce-scatter.3.cloned.1.call-update) | async-done | bytes 3670032 | tf_op jit(solution)/shard_map/reduce_scatter | solution.py:58
  127.3 14.3 %subtract_convert_fusion = (bf16[1792,1024]{1,0:T(8,128)(2,1)}, f32[1792,1024]{1,0:T(8,128)}) fusion(f32[1792,1024]{1,0:T(8,128)} %param.11, f32[1792,1024]{1,0:T(8,128)} %param.13, bf16[1792,1024]{1,0:T(8,128)(2,1)} %reduce-scatter.3.cloned.1.call-done, f32[1792,1024]{1,0:T(8,128)} %param.12), kind=kLoop, calls=%fused_computation.24 | loop fusion | flops 33030144 | bytes 36700160 | tf_op jit(solution)/shard_map/convert_element_type | solution.py:65
  142.9 6.1 copy.11
  149.0 551.7 %all-gather.3.cloned.1.call-done = bf16[14336,1024]{1,0:T(8,128)(2,1)} async-done(((bf16[1792,1024]{1,0:T(8,128)(2,1)}), bf16[14336,1024]{1,0:T(8,128)(2,1)}) %all-gather.3.cloned.1.call-update) | async-done | bytes 29360144 | tf_op jit(solution)/shard_map/all_gather | solution.py:73
  700.8 10.1 %convert_bitcast_fusion = f32[2,224,8,1024]{3,2,1,0:T(8,128)} fusion(bf16[8,1792,1024]{2,1,0:T(8,128)(2,1)} %bitcast.41, s32[]{:T(128)S(6)} %select_n.11), kind=kLoop, calls=%fused_computation.8 | loop fusion | flops 3670016 | bytes 22020100
  710.9 13.6 %copy.15 = f32[2,224,8,1024]{3,2,0,1:T(8,128)} copy(f32[2,224,8,1024]{3,2,1,0:T(8,128)} %convert_bitcast_fusion) | data formatting | bytes 29360128 | tf_op jit(solution)/shard_map/convert_element_type | solution.py:76
  724.5 18.8 %abs_bitcast_fusion = (f32[224,8,16,128]{3,1,2,0:T(8,128)}, f32[1792,2048]{1,0:T(8,128)}) fusion(f32[1792,2048]{1,0:T(8,128)} %bitcast.37, bf16[1792,2048]{1,0:T(8,128)(2,1)} %param.14), kind=kLoop, calls=%fused_computation.10 | loop fusion | flops 11010048 | bytes 51380224
  743.3 14.0 %copy.16 = f32[224,8,16,128]{3,2,1,0:T(8,128)} copy(f32[224,8,16,128]{3,1,2,0:T(8,128)} %get-tuple-element.63) | data formatting | bytes 29360128
  763.4 9.1 multiply_convert_fusion
  772.5 113.2 %while.11 = (s32[]{:T(128)}, f32[1024,2048]{1,0:T(8,128)}, bf16[14,1024,128]{1,2,0:T(8,128)(2,1)}, bf16[14,128,2048]{2,1,0:T(8,128)(2,1)}, f32[14,2048]{1,0:T(8,128)S(1)}, /*index=5*/s32[]{:T(128)}, s32[]{:T(128)}) while((s32[]{:T(128)}, f32[1024,2048]{1,0:T(8,128)}, bf16[14,1024,128]{1,2,0:T(8,128)(2,1)}, ...), condition=%wide.region_3.4_spmd.clone, body=%wide.region_2.3_spmd.clone.sunk | while | flops 543162368 | bytes 17589336 | solution.py:44
  778.3 8.2 select_add_fusion.2
  786.5 8.2 select_add_fusion.2
  794.8 8.2 select_add_fusion.2
  803.1 8.2 select_add_fusion.2
  811.3 8.2 select_add_fusion.2
  819.6 8.2 select_add_fusion.2
  827.8 8.2 select_add_fusion.2
  836.1 8.2 select_add_fusion.2
  844.4 8.2 select_add_fusion.2
  852.6 8.2 select_add_fusion.2
  860.9 8.2 select_add_fusion.2
  869.2 8.2 select_add_fusion.2
  877.4 8.2 select_add_fusion.2
  892.3 43.9 %reduce-scatter.5.cloned.1.call-done = bf16[1024,512]{1,0:T(8,128)(2,1)} async-done(((bf16[1024,2048]{1,0:T(8,128)(2,1)}), bf16[1024,512]{1,0:T(8,128)(2,1)}) %reduce-scatter.5.cloned.1.call-update) | async-done | bytes 1048592 | tf_op jit(solution)/shard_map/reduce_scatter | solution.py:78
  (33 shorter events, 21.9 us)
Async XLA Ops:
  7.2 120.1 %reduce-scatter.3.cloned.1.call-start = ((), (), s32[]{:S(2)}) async-start(), calls=%async_computation.2 | async-start | bytes 18350080 | tf_op jit(solution)/shard_map/reduce_scatter | solution.py:58
  7.9 133.7 %copy-start = (s32[8]{0:T(128)S(1)}, s32[8]{0:T(128)}, u32[]{:S(2)}) copy-start(s32[8]{0:T(128)} %param.16) | copy-start | bytes 100
  7.9 692.8 %all-gather.3.cloned.1.call-start = ((), (), s32[]{:S(2)}) async-start(), calls=%async_computation.4 | async-start | bytes 33030144 | tf_op jit(solution)/shard_map/all_gather | solution.py:73
  141.6 794.6 %reduce-scatter.5.cloned.1.call-start = ((), (), s32[]{:S(2)}) async-start(), calls=%async_computation.3 | async-start | bytes 5242880 | tf_op jit(solution)/shard_map/reduce_scatter | solution.py:78
Sparse Core Ops, SparseCore 0:
  10.6 116.6 reduce-scatter.2
  141.7 559.0 all-gather.2
  891.8 44.3 reduce-scatter.4
where the time goes:
time: 946 us; the launch traced here: 945 us
  waiting for transfers between devices  716 us (76%)
  matrix products  113 us (12%)
  other arithmetic  66.7 us (7%)
  local copies, waits for them, and re-layouts  34.6 us (4%)
  between operations  15.1 us (2%)
    all_gather x1, waiting for transfers between devices, body(): gathered = lax.all_gather(delta[None], 'expert', axis=0, tiled=True)  552 us
    reduce_scatter x1, waiting for transfers between devices, body(): lax.psum_scatter(grad_partials[0].astype(jnp.float32).astype(jnp.bfloat16...  119 us
    dot_general x14, matrix products, step_block(): jnp.dot(tile_part, weight_part, preferred_element_type=jnp.float32)  113 us
    reduce_scatter x1, waiting for transfers between devices, body(): lax.psum_scatter(partial_out.astype(jnp.bfloat16), 'dp', scatter_dimensio...  43.9 us
    unnamed x3, other arithmetic  28.9 us
    unnamed x6, local copies, waits for them, and re-layouts  20.2 us
  transfers between devices with their start and end apart: 3, of which 3 were waited for; matrix products, arithmetic and copies ran while one was open for 1% of the time, Pallas kernels for 0%

commit v1 on v0

--- a/solution.py
+++ b/solution.py
@@ -70,7 +70,19 @@
     depth_blocks = token_tiles.shape[1] // QB
     stacked = token_tiles.reshape(rows_local, depth_blocks, QB).transpose(1, 0, 2)
     part_cols = delta.shape[1]
-    gathered = lax.all_gather(delta[None], "expert", axis=0, tiled=True)
+
+    def check_the_things(slab_in, mesh_ax):
+        lanes = lax.psum(1, axis_name=mesh_ax)
+        near = [None] * lanes
+        near[lanes - 1] = slab_in
+        arrivals = tuple(((u, (u + 1) % lanes) for u in range(lanes)))
+        for pp in range(lanes - 2, -1, -1):
+            near[pp] = lax.ppermute(near[pp + 1], axis_name=mesh_ax, perm=arrivals)
+        return jnp.roll(
+            jnp.concatenate(near, axis=0), (lax.axis_index(mesh_ax) + 1) * slab_in.shape[0], axis=0
+        )
+
+    gathered = check_the_things(delta[None], "expert")
     own_pieces = lax.dynamic_slice_in_dim(gathered, own_expert * group_size, group_size, 0)
     change = own_pieces.transpose(1, 0, 2).reshape(own_pieces.shape[1], group_size * part_cols)
     weight = resident_weights.astype(jnp.float32) + change.astype(jnp.float32)

time: 946 us -> 1020 us (1.078)
  local copies, waits for them, and re-layouts: 34.6 us -> 156 us
  waiting for transfers between devices: 716 us -> 668 us
    all_gather x1 -> x0, waiting for transfers between devices: 552 us -> none  [body(): gathered = lax.all_gather(delta[None], 'expert', axis=0, tiled=True)]
    ppermute x0 -> x7, waiting for transfers between devices: none -> 549 us  [check_the_things(): near[pp] = lax.ppermute(near[pp + 1], axis_name=mesh_ax, perm=arrivals)]
    unnamed x6 -> x55, local copies, waits for them, and re-layouts: 20.2 us -> 121 us
    reduce_scatter x1, waiting for transfers between devices: 119 us -> 86.4 us  [body(): lax.psum_scatter(grad_partials[0].astype(jnp.float32).astype(jnp.bfloat16...]
    unnamed x3 -> x2, other arithmetic: 28.9 us -> 0.01 us
    abs x0 -> x1, local copies, waits for them, and re-layouts: none -> 16.9 us  [block_product(): largest = jnp.max(jnp.abs(blocks), axis=(1, 3))]
    add x0 -> x1, local copies, waits for them, and re-layouts: none -> 15.3 us  [body(): weight = resident_weights.astype(jnp.float32) + change.astype(jnp.float32)]
    abs x0 -> x1, other arithmetic: none -> 14.6 us  [block_product(): largest = jnp.max(jnp.abs(blocks), axis=(1, 3))]
  transfers between devices with their start and end apart: 3 -> 9, of which waited for: 3 -> 9; matrix products, arithmetic and copies ran while one was open for 1% -> 5% of each run, Pallas kernels for 0% -> 0%
where the time goes in v1:
time: 1020 us
  waiting for transfers between devices  668 us (65%)
  local copies, waits for them, and re-layouts  156 us (15%)
  matrix products  114 us (11%)
  other arithmetic  62.5 us (6%)
  between operations  15.4 us (2%)
    ppermute x7, waiting for transfers between devices, check_the_things(): near[pp] = lax.ppermute(near[pp + 1], axis_name=mesh_ax, perm=arrivals)  549 us
    unnamed x55, local copies, waits for them, and re-layouts  121 us
    dot_general x14, matrix products, step_block(): jnp.dot(tile_part, weight_part, preferred_element_type=jnp.float32)  114 us
    reduce_scatter x1, waiting for transfers between devices, body(): lax.psum_scatter(grad_partials[0].astype(jnp.float32).astype(jnp.bfloat16...  86.4 us
    reduce_scatter x1, waiting for transfers between devices, body(): lax.psum_scatter(partial_out.astype(jnp.bfloat16), 'dp', scatter_dimensio...  32.8 us
  transfers between devices with their start and end apart: 9, of which 9 were waited for; matrix products, arithmetic and copies ran while one was open for 5% of the time, Pallas kernels for 0%

profile of v1, /device:TPU:0, one launch (start us, length us, event | category | flops | bytes accessed | tf_op | source)
XLA Modules:
  0.0 1017.6 jit_solution(6832132402945634980)
XLA Ops:
  7.2 18.5 %copy.22 = bf16[1,7168,1024]{1,2,0:T(8,128)(2,1)} copy(bf16[1,7168,1024]{2,1,0:T(8,128)(2,1)} %param.10) | data formatting | bytes 29360128 | tf_op args[0]
  25.8 8.4 copy.21
  34.2 9.4 copy.23
  43.6 8.6 copy.25
  52.3 86.4 %reduce-scatter.3.cloned.1.call-done = bf16[1792,1024]{0,1:T(8,128)(2,1)} async-done(((bf16[7168,1024]{0,1:T(8,128)(2,1)}), bf16[1792,1024]{0,1:T(8,128)(2,1)}) %reduce-scatter.3.cloned.1.call-update) | async-done | bytes 3670032 | tf_op jit(solution)/shard_map/reduce_scatter | solution.py:58
  138.7 13.7 %fusion.15 = (bf16[1,1792,1024]{1,2,0:T(8,128)(2,1)S(1)}, f32[1792,1024]{0,1:T(8,128)}) fusion(f32[1792,1024]{0,1:T(8,128)} %copy.25, f32[1792,1024]{0,1:T(8,128)} %copy.23, bf16[1792,1024]{0,1:T(8,128)(2,1)} %reduce-scatter.3.cloned.1.call-done, f32[1792,1024]{0,1:T(8,128)} %copy.21), kind=kLoop, calls=%fused_computation.23 | loop fusion | flops 33030144 | bytes 36700160 | tf_op jit(solution)/shard_map/broadcast_in_dim | solution.py:85
  155.6 82.1 %collective-permute-done = bf16[1,1792,1024]{1,2,0:T(8,128)(2,1)S(1)} collective-permute-done((bf16[1,1792,1024]{1,2,0:T(8,128)(2,1)S(1)}, bf16[1,1792,1024]{1,2,0:T(8,128)(2,1)S(1)}, u32[]{:S(2)}, u32[]{:S(2)}) %collective-permute-start) | collective-permute-done | bytes 3670048 | tf_op jit(solution)/shard_map/ppermute | solution.py:80
  239.6 82.7 %collective-permute-done.1 = bf16[1,1792,1024]{1,2,0:T(8,128)(2,1)S(1)} collective-permute-done((bf16[1,1792,1024]{1,2,0:T(8,128)(2,1)S(1)}, bf16[1,1792,1024]{1,2,0:T(8,128)(2,1)S(1)}, u32[]{:S(2)}, u32[]{:S(2)}) %collective-permute-start.1) | collective-permute-done | bytes 3670048 | tf_op jit(solution)/shard_map/ppermute | solution.py:80
  324.2 81.9 %collective-permute-done.2 = bf16[1,1792,1024]{1,2,0:T(8,128)(2,1)S(1)} collective-permute-done((bf16[1,1792,1024]{1,2,0:T(8,128)(2,1)S(1)}, bf16[1,1792,1024]{1,2,0:T(8,128)(2,1)S(1)}, u32[]{:S(2)}, u32[]{:S(2)}) %collective-permute-start.2) | collective-permute-done | bytes 3670048 | tf_op jit(solution)/shard_map/ppermute | solution.py:80
  407.8 81.0 %collective-permute-done.3 = bf16[1,1792,1024]{1,2,0:T(8,128)(2,1)S(1)} collective-permute-done((bf16[1,1792,1024]{1,2,0:T(8,128)(2,1)S(1)}, bf16[1,1792,1024]{1,2,0:T(8,128)(2,1)S(1)}, u32[]{:S(2)}, u32[]{:S(2)}) %collective-permute-start.3) | collective-permute-done | bytes 3670048 | tf_op jit(solution)/shard_map/ppermute | solution.py:80
  490.7 80.2 %collective-permute-done.4 = bf16[1,1792,1024]{1,2,0:T(8,128)(2,1)S(1)} collective-permute-done((bf16[1,1792,1024]{1,2,0:T(8,128)(2,1)S(1)}, bf16[1,1792,1024]{1,2,0:T(8,128)(2,1)S(1)}, u32[]{:S(2)}, u32[]{:S(2)}) %collective-permute-start.4) | collective-permute-done | bytes 3670048 | tf_op jit(solution)/shard_map/ppermute | solution.py:80
  572.6 79.4 %collective-permute-done.5 = bf16[1,1792,1024]{1,2,0:T(8,128)(2,1)} collective-permute-done((bf16[1,1792,1024]{1,2,0:T(8,128)(2,1)S(1)}, bf16[1,1792,1024]{1,2,0:T(8,128)(2,1)}, u32[]{:S(2)}, u32[]{:S(2)}) %collective-permute-start.5) | collective-permute-done | bytes 3670048 | tf_op jit(solution)/shard_map/ppermute | solution.py:80
  653.3 9.9 copy.27
  669.2 61.6 %collective-permute-done.6 = bf16[1,1792,1024]{1,2,0:T(8,128)(2,1)} collective-permute-done((bf16[1,1792,1024]{1,2,0:T(8,128)(2,1)}, bf16[1,1792,1024]{1,2,0:T(8,128)(2,1)}, u32[]{:S(2)}, u32[]{:S(2)}) %collective-permute-start.6) | collective-permute-done | bytes 3670048 | tf_op jit(solution)/shard_map/ppermute | solution.py:80
  773.1 9.9 dynamic-slice_convert_fusion
  783.0 14.6 %fusion.16 = (f32[1792,2048]{0,1:T(8,128)}, f32[1792,2048]{0,1:T(8,128)}) fusion(f32[2,1792,1024]{1,2,0:T(8,128)} %dynamic-slice_convert_fusion, bf16[1792,2048]{0,1:T(8,128)(2,1)S(1)} %bitcast.37), kind=kLoop, calls=%fused_computation.43 | loop fusion | flops 11010048 | bytes 51380224 | tf_op jit(solution)/shard_map/abs | solution.py:31
  797.6 16.9 %reshape.27 = f32[14,128,16,128]{1,0,3,2:T(8,128)} reshape(f32[1792,2048]{0,1:T(8,128)} %get-tuple-element.72) | data formatting | bytes 29360128 | tf_op jit(solution)/shard_map/abs | solution.py:31
  821.6 15.3 %copy.29 = f32[1792,2048]{1,0:T(8,128)} copy(f32[1792,2048]{0,1:T(8,128)} %get-tuple-element.73) | data formatting | bytes 29360128 | tf_op jit(solution)/shard_map/add | solution.py:88
  836.8 9.0 multiply_convert_fusion
  845.9 114.2 %while.11 = (s32[]{:T(128)}, f32[1024,2048]{1,0:T(8,128)}, bf16[14,1024,128]{1,2,0:T(8,128)(2,1)}, bf16[14,128,2048]{2,1,0:T(8,128)(2,1)}, f32[14,2048]{1,0:T(8,128)S(1)}, /*index=5*/s32[]{:T(128)}, s32[]{:T(128)}) while((s32[]{:T(128)}, f32[1024,2048]{1,0:T(8,128)}, bf16[14,1024,128]{1,2,0:T(8,128)(2,1)}, ...), condition=%wide.region_3.4_spmd.clone, body=%wide.region_2.3_spmd.clone.sunk | while | flops 543162368 | bytes 17589336 | solution.py:44
  851.7 8.3 select_add_fusion.2
  876.7 8.3 select_add_fusion.2
  966.8 8.7 copy.32
  975.5 32.8 %reduce-scatter.5.cloned.1.call-done = bf16[1024,512]{1,0:T(8,128)(2,1)} async-done(((bf16[1024,2048]{1,0:T(8,128)(2,1)}), bf16[1024,512]{1,0:T(8,128)(2,1)}) %reduce-scatter.5.cloned.1.call-update) | async-done | bytes 1048592 | tf_op jit(solution)/shard_map/reduce_scatter | solution.py:90
  (96 shorter events, 174.3 us)
Async XLA Ops:
  7.2 131.5 %reduce-scatter.3.cloned.1.call-start = ((), (), s32[]{:S(2)}) async-start(), calls=%async_computation.2 | async-start | bytes 18350080 | tf_op jit(solution)/shard_map/reduce_scatter | solution.py:58
  25.7 982.6 %reduce-scatter.5.cloned.1.call-start = ((), (), s32[]{:S(2)}) async-start(), calls=%async_computation.3 | async-start | bytes 5242880 | tf_op jit(solution)/shard_map/reduce_scatter | solution.py:90
  52.3 599.8 %copy-start.12 = (s32[8]{0:T(128)S(1)}, s32[8]{0:T(128)}, u32[]{:S(2)}) copy-start(s32[8]{0:T(128)} %param.16) | copy-start | bytes 100
  152.4 1.8 copy-start
  154.1 83.6 %collective-permute-start = (bf16[1,1792,1024]{1,2,0:T(8,128)(2,1)S(1)}, bf16[1,1792,1024]{1,2,0:T(8,128)(2,1)S(1)}, u32[]{:S(2)}, u32[]{:S(2)}) collective-permute-start(bf16[1,1792,1024]{1,2,0:T(8,128)(2,1)S(1)} %get-tuple-element.74), channel_id=1, source_target_pairs={{0,1},{1,2},{2,3},{3,4},{4,5},{5,6},{6,7},{7,0},{8,9},{9,10},{10,1... | collective-permute-start | bytes 11010056 | tf_op jit(solution)/shard_map/ppermute | solution.py:80
  237.7 1.9 copy-start.2
  239.6 82.7 %collective-permute-start.1 = (bf16[1,1792,1024]{1,2,0:T(8,128)(2,1)S(1)}, bf16[1,1792,1024]{1,2,0:T(8,128)(2,1)S(1)}, u32[]{:S(2)}, u32[]{:S(2)}) collective-permute-start(bf16[1,1792,1024]{1,2,0:T(8,128)(2,1)S(1)} %collective-permute-done), channel_id=1, source_target_pairs={{0,1},{1,2},{2,3},{3,4},{4,5},{5,6},{6,7},{7,0},{8,9},{9,10},{10,1... | collective-permute-start | bytes 11010056 | tf_op jit(solution)/shard_map/ppermute | solution.py:80
  322.4 1.8 copy-start.4
  324.2 81.9 %collective-permute-start.2 = (bf16[1,1792,1024]{1,2,0:T(8,128)(2,1)S(1)}, bf16[1,1792,1024]{1,2,0:T(8,128)(2,1)S(1)}, u32[]{:S(2)}, u32[]{:S(2)}) collective-permute-start(bf16[1,1792,1024]{1,2,0:T(8,128)(2,1)S(1)} %collective-permute-done.1), channel_id=1, source_target_pairs={{0,1},{1,2},{2,3},{3,4},{4,5},{5,6},{6,7},{7,0},{8,9},{9,10},{10,1... | collective-permute-start | bytes 11010056 | tf_op jit(solution)/shard_map/ppermute | solution.py:80
  406.1 1.8 copy-start.6
  407.8 81.0 %collective-permute-start.3 = (bf16[1,1792,1024]{1,2,0:T(8,128)(2,1)S(1)}, bf16[1,1792,1024]{1,2,0:T(8,128)(2,1)S(1)}, u32[]{:S(2)}, u32[]{:S(2)}) collective-permute-start(bf16[1,1792,1024]{1,2,0:T(8,128)(2,1)S(1)} %collective-permute-done.2), channel_id=1, source_target_pairs={{0,1},{1,2},{2,3},{3,4},{4,5},{5,6},{6,7},{7,0},{8,9},{9,10},{10,1... | collective-permute-start | bytes 11010056 | tf_op jit(solution)/shard_map/ppermute | solution.py:80
  488.9 1.8 copy-start.8
  490.7 80.2 %collective-permute-start.4 = (bf16[1,1792,1024]{1,2,0:T(8,128)(2,1)S(1)}, bf16[1,1792,1024]{1,2,0:T(8,128)(2,1)S(1)}, u32[]{:S(2)}, u32[]{:S(2)}) collective-permute-start(bf16[1,1792,1024]{1,2,0:T(8,128)(2,1)S(1)} %collective-permute-done.3), channel_id=1, source_target_pairs={{0,1},{1,2},{2,3},{3,4},{4,5},{5,6},{6,7},{7,0},{8,9},{9,10},{10,1... | collective-permute-start | bytes 11010056 | tf_op jit(solution)/shard_map/ppermute | solution.py:80
  570.8 1.8 copy-start.10
  572.6 79.4 %collective-permute-start.5 = (bf16[1,1792,1024]{1,2,0:T(8,128)(2,1)S(1)}, bf16[1,1792,1024]{1,2,0:T(8,128)(2,1)}, u32[]{:S(2)}, u32[]{:S(2)}) collective-permute-start(bf16[1,1792,1024]{1,2,0:T(8,128)(2,1)S(1)} %collective-permute-done.4), channel_id=1, source_target_pairs={{0,1},{1,2},{2,3},{3,4},{4,5},{5,6},{6,7},{7,0},{8,9},{9,10},{10,1... | collective-permute-start | bytes 11010056 | tf_op jit(solution)/shard_map/ppermute | solution.py:80
  652.0 78.8 %collective-permute-start.6 = (bf16[1,1792,1024]{1,2,0:T(8,128)(2,1)}, bf16[1,1792,1024]{1,2,0:T(8,128)(2,1)}, u32[]{:S(2)}, u32[]{:S(2)}) collective-permute-start(bf16[1,1792,1024]{1,2,0:T(8,128)(2,1)} %collective-permute-done.5), channel_id=1, source_target_pairs={{0,1},{1,2},{2,3},{3,4},{4,5},{5,6},{6,7},{7,0},{8,9},{9,10},{10,1... | collective-permute-start | bytes 11010056 | tf_op jit(solution)/shard_map/ppermute | solution.py:80
  669.2 69.9 %copy-start.11 = (bf16[1,1792,1024]{1,2,0:T(8,128)(2,1)S(1)}, bf16[1,1792,1024]{1,2,0:T(8,128)(2,1)}, u32[]{:S(2)}) copy-start(bf16[1,1792,1024]{1,2,0:T(8,128)(2,1)} %copy-done.10) | copy-start | bytes 11010052
  734.9 6.4 copy-start.9
  739.1 4.3 copy-start.7
  741.3 4.4 copy-start.5
  743.5 4.8 copy-start.3
  745.7 4.6 copy-start.1
  771.0 12.0 %slice-start = ((s8[7340032]{0:T(1024)(128)(4,1)}), s8[4194304]{0:T(1024)(128)(4,1)S(1)}, s32[]{:S(2)}) async-start(s8[7340032]{0:T(1024)(128)(4,1)} %bitcast.36), calls=%async_computation.4 | async-start | bytes 8388608
  773.1 9.9 slice-start.1
Sparse Core Ops, SparseCore 0:
  25.9 112.8 reduce-scatter.2
  966.3 41.9 reduce-scatter.4
